TPU v7x, 32 devices: a whole 2x2x4 slice. The times are simulated.
32 devices in a mesh: fsdp: 16 (over z, y, core), seq: 2 (over x).
Axes of the slice: x: 2, y: 2, z: 4, core: 2. Of those that a mesh axis runs over, the one named last changes fastest.
Arguments:
- tokens: bfloat16 [16, 1024, 1024], P('fsdp', 'seq'), may hold values from -6 to 6
- condition: bfloat16 [16, 1024], P('fsdp'), may hold values from -6 to 6
- w_ada: bfloat16 [1024, 6144], P('fsdp'), may hold values from -0.1875 to 0.1875
- b_ada: bfloat16 [6144], P('fsdp'), may hold values from -3 to 3
- w_qkv: bfloat16 [1024, 3072], P('fsdp'), may hold values from -0.1875 to 0.1875
- b_qv: bfloat16 [2048], P('fsdp'), may hold values from -1.1953125 to 1.1953125
- w_proj: bfloat16 [1024, 1024], P('fsdp'), may hold values from -0.1875 to 0.1875
- b_proj: bfloat16 [1024], P('fsdp'), may hold values from -1.1953125 to 1.1953125
- w_fc1: bfloat16 [1024, 4096], P('fsdp'), may hold values from -0.1875 to 0.1875
- b_fc1: bfloat16 [4096], P('fsdp'), may hold values from -1.1953125 to 1.1953125
- w_fc2: bfloat16 [4096, 1024], P('fsdp'), may hold values from -0.09375 to 0.09375
- b_fc2: bfloat16 [1024], P('fsdp'), may hold values from -1.1953125 to 1.1953125
- cotangent: bfloat16 [16, 1024, 1024], P('fsdp', 'seq'), may hold values from -6 to 6
Outputs:
- out_tokens: bfloat16 [16, 1024, 1024], P('fsdp', 'seq')
- grad_tokens: float32 [16, 1024, 1024], P('fsdp', 'seq')
- grad_condition: float32 [16, 1024], P('fsdp')
- grad_w_ada: float32 [1024, 6144], P('fsdp')
- grad_b_ada: float32 [6144], P('fsdp')
- grad_w_qkv: float32 [1024, 3072], P('fsdp')
- grad_b_qv: float32 [2048], P('fsdp')
- grad_w_proj: float32 [1024, 1024], P('fsdp')
- grad_b_proj: float32 [1024], P('fsdp')
- grad_w_fc1: float32 [1024, 4096], P('fsdp')
- grad_b_fc1: float32 [4096], P('fsdp')
- grad_w_fc2: float32 [4096, 1024], P('fsdp')
- grad_b_fc2: float32 [1024], P('fsdp')
All inputs are finite; a program needn't handle non-finite values.
Results may differ from a plain program's by a relative error of at most 0.018.
The roundings to bfloat16 on the way count: a program that leaves them out, or rounds other values in their place, can miss the bound.
Values may be sent and summed in bfloat16 or wider, within the bound.
A program may use at most 256 MiB of HBM per device.

v0:
```python
from functools import partial
import jax
import jax.numpy as jnp
from jax import lax
from jax.sharding import PartitionSpec as P

HD = 64
norm_eps = 1e-06
block_rows = 512


def layer_norm(values):
    center = values - jnp.mean(values, axis=-1, keepdims=True)
    rscale = lax.rsqrt(jnp.mean(center * center, axis=-1, keepdims=True) + norm_eps)
    return (center * rscale, rscale)


def norm_back(upstream, normed, rscale):
    mean_up = jnp.mean(upstream, axis=-1, keepdims=True)
    mean_cross = jnp.mean(upstream * normed, axis=-1, keepdims=True)
    return rscale * (upstream - mean_up - normed * mean_cross)


def attend_forward(queries, keys_all, values_all):
    seq_len = keys_all.shape[1]
    rows = min(block_rows, seq_len)
    score_scale = queries.shape[-1] ** (-0.5)
    outputs = []
    totals = []
    for offset in range(0, seq_len, rows):
        q_block = queries[:, offset : offset + rows]
        raw_scores = jnp.einsum(
            "bqhd,bkhd->bhqk", q_block, keys_all, preferred_element_type=jnp.float32
        )
        scores = raw_scores * score_scale
        row_max = jnp.max(scores, axis=-1, keepdims=True)
        shifted = jnp.exp(scores - row_max)
        row_total = jnp.sum(shifted, axis=-1, keepdims=True)
        attn_prob = (shifted / row_total).astype(jnp.bfloat16)
        block_out = jnp.einsum(
            "bhqk,bkhd->bqhd", attn_prob, values_all, preferred_element_type=jnp.float32
        )
        outputs.append(block_out.astype(jnp.bfloat16))
        totals.append(row_max + jnp.log(row_total))
    return (jnp.concatenate(outputs, axis=1), jnp.concatenate(totals, axis=2))


def attend_backward(queries, keys_all, values_all, log_total, d_out):
    seq_len = keys_all.shape[1]
    rows = min(block_rows, seq_len)
    score_scale = queries.shape[-1] ** (-0.5)
    grad_keys = jnp.zeros(keys_all.shape, jnp.float32)
    grad_values = jnp.zeros(values_all.shape, jnp.float32)
    grad_queries = []
    for offset in range(0, seq_len, rows):
        q_block = queries[:, offset : offset + rows]
        d_block = d_out[:, offset : offset + rows]
        raw_scores = jnp.einsum(
            "bqhd,bkhd->bhqk", q_block, keys_all, preferred_element_type=jnp.float32
        )
        attn_prob = jnp.exp(raw_scores * score_scale - log_total[:, :, offset : offset + rows])
        grad_values = grad_values + jnp.einsum(
            "bhqk,bqhd->bkhd",
            attn_prob.astype(jnp.bfloat16),
            d_block,
            preferred_element_type=jnp.float32,
        )
        d_prob = jnp.einsum(
            "bqhd,bkhd->bhqk", d_block, values_all, preferred_element_type=jnp.float32
        )
        center = jnp.sum(attn_prob * d_prob, axis=-1, keepdims=True)
        d_raw = (attn_prob * (d_prob - center) * score_scale).astype(jnp.bfloat16)
        grad_queries.append(
            jnp.einsum("bhqk,bkhd->bqhd", d_raw, keys_all, preferred_element_type=jnp.float32)
        )
        grad_keys = grad_keys + jnp.einsum(
            "bhqk,bqhd->bkhd", d_raw, q_block, preferred_element_type=jnp.float32
        )
    grad_q = jnp.concatenate(grad_queries, axis=1).astype(jnp.bfloat16)
    return (grad_q, grad_keys.astype(jnp.bfloat16), grad_values.astype(jnp.bfloat16))


def on_device(
    tokens,
    condition,
    w_ada,
    b_ada,
    w_qkv,
    b_qv,
    w_proj,
    b_proj,
    w_fc1,
    b_fc1,
    w_fc2,
    b_fc2,
    cotangent,
):
    latents, local_len, model_width = tokens.shape
    groups = lax.axis_size("seq")
    head_dim = HD
    group_width = model_width // groups
    per_group = group_width // head_dim
    ada_w, ada_b, qkv_w, qv_b, proj_w, proj_b, fc1_w, fc1_b, fc2_w, fc2_b = (
        lax.all_gather(w_ada, "fsdp", axis=0, tiled=True),
        lax.all_gather(b_ada, "fsdp", axis=0, tiled=True),
        lax.all_gather(w_qkv, "fsdp", axis=0, tiled=True),
        lax.all_gather(b_qv, "fsdp", axis=0, tiled=True),
        lax.all_gather(w_proj, "fsdp", axis=0, tiled=True),
        lax.all_gather(b_proj, "fsdp", axis=0, tiled=True),
        lax.all_gather(w_fc1, "fsdp", axis=0, tiled=True),
        lax.all_gather(b_fc1, "fsdp", axis=0, tiled=True),
        lax.all_gather(w_fc2, "fsdp", axis=0, tiled=True),
        lax.all_gather(b_fc2, "fsdp", axis=0, tiled=True),
    )
    tokens_f = tokens.astype(jnp.float32)
    lifted, silu_back = jax.vjp(jax.nn.silu, condition.astype(jnp.float32))
    lifted_b = lifted.astype(jnp.bfloat16)
    modulation = jnp.dot(lifted_b, ada_w, preferred_element_type=jnp.float32) + ada_b.astype(
        jnp.float32
    )
    shift_one, scale_one, gate_one, shift_two, scale_two, gate_two = jnp.split(
        modulation[:, None, :], 6, axis=-1
    )
    normed_one, rscale_one = layer_norm(tokens_f)
    hidden_one = (normed_one * (1.0 + scale_one) + shift_one).astype(jnp.bfloat16)
    qkv_bias = jnp.concatenate(
        [qv_b[:model_width], jnp.zeros((model_width,), jnp.bfloat16), qv_b[model_width:]]
    ).astype(jnp.float32)
    qkv_tok = (jnp.dot(hidden_one, qkv_w, preferred_element_type=jnp.float32) + qkv_bias).astype(
        jnp.bfloat16
    )
    spread = lax.all_to_all(
        qkv_tok.reshape(latents, local_len, 3, groups, group_width),
        "seq",
        split_axis=3,
        concat_axis=1,
        tiled=True,
    )
    seq_len = spread.shape[1]
    queries = spread[:, :, 0, 0].reshape(latents, seq_len, per_group, head_dim)
    keys_all = spread[:, :, 1, 0].reshape(latents, seq_len, per_group, head_dim)
    values_all = spread[:, :, 2, 0].reshape(latents, seq_len, per_group, head_dim)
    attn_out, log_total = attend_forward(queries, keys_all, values_all)
    returned = lax.all_to_all(
        attn_out.reshape(latents, seq_len, 1, group_width),
        "seq",
        split_axis=1,
        concat_axis=2,
        tiled=True,
    )
    attn_tok = returned.reshape(latents, local_len, model_width)
    branch = jnp.dot(attn_tok, proj_w, preferred_element_type=jnp.float32) + proj_b.astype(
        jnp.float32
    )
    middle = tokens_f + gate_one * branch
    normed_two, rscale_two = layer_norm(middle)
    hidden_two = (normed_two * (1.0 + scale_two) + shift_two).astype(jnp.bfloat16)
    pre_act = jnp.dot(hidden_two, fc1_w, preferred_element_type=jnp.float32) + fc1_b.astype(
        jnp.float32
    )
    act_f, gelu_back = jax.vjp(partial(jax.nn.gelu, approximate=True), pre_act)
    act_b = act_f.astype(jnp.bfloat16)
    mlp_out = jnp.dot(act_b, fc2_w, preferred_element_type=jnp.float32) + fc2_b.astype(jnp.float32)
    result = (middle + gate_two * mlp_out).astype(jnp.bfloat16)
    grad_out = cotangent.astype(jnp.float32)
    d_gate_two = jnp.sum(grad_out * mlp_out, axis=1)
    d_mlp = (grad_out * gate_two).astype(jnp.bfloat16)
    grad_fc2 = jnp.einsum("btf,btd->fd", act_b, d_mlp, preferred_element_type=jnp.float32)
    bias_fc2 = jnp.sum(d_mlp, axis=(0, 1), dtype=jnp.float32)
    d_act = jnp.einsum("btd,fd->btf", d_mlp, fc2_w, preferred_element_type=jnp.float32)
    d_pre = gelu_back(d_act)[0].astype(jnp.bfloat16)
    grad_fc1 = jnp.einsum("btd,btf->df", hidden_two, d_pre, preferred_element_type=jnp.float32)
    bias_fc1 = jnp.sum(d_pre, axis=(0, 1), dtype=jnp.float32)
    d_hidden_two = jnp.einsum("btf,df->btd", d_pre, fc1_w, preferred_element_type=jnp.float32)
    d_shift_two = jnp.sum(d_hidden_two, axis=1)
    d_scale_two = jnp.sum(d_hidden_two * normed_two, axis=1)
    d_middle = grad_out + norm_back(d_hidden_two * (1.0 + scale_two), normed_two, rscale_two)
    d_gate_one = jnp.sum(d_middle * branch, axis=1)
    d_branch = (d_middle * gate_one).astype(jnp.bfloat16)
    grad_proj = jnp.einsum("btk,btd->kd", attn_tok, d_branch, preferred_element_type=jnp.float32)
    bias_proj = jnp.sum(d_branch, axis=(0, 1), dtype=jnp.float32)
    d_attn = jnp.einsum("btd,kd->btk", d_branch, proj_w, preferred_element_type=jnp.float32).astype(
        jnp.bfloat16
    )
    d_heads = lax.all_to_all(
        d_attn.reshape(latents, local_len, groups, group_width),
        "seq",
        split_axis=2,
        concat_axis=1,
        tiled=True,
    )
    d_heads = d_heads.reshape(latents, seq_len, per_group, head_dim)
    grad_q, grad_k, grad_v = attend_backward(queries, keys_all, values_all, log_total, d_heads)
    d_spread = jnp.stack([grad_q, grad_k, grad_v], axis=2).reshape(
        latents, seq_len, 3, 1, group_width
    )
    d_qkv = lax.all_to_all(d_spread, "seq", split_axis=1, concat_axis=3, tiled=True).reshape(
        latents, local_len, 3 * model_width
    )
    grad_qkv = jnp.einsum("btd,bte->de", hidden_one, d_qkv, preferred_element_type=jnp.float32)
    column_sums = jnp.sum(d_qkv, axis=(0, 1), dtype=jnp.float32)
    bias_qv = jnp.concatenate([column_sums[:model_width], column_sums[2 * model_width :]])
    d_hidden_one = jnp.einsum("bte,de->btd", d_qkv, qkv_w, preferred_element_type=jnp.float32)
    d_shift_one = jnp.sum(d_hidden_one, axis=1)
    d_scale_one = jnp.sum(d_hidden_one * normed_one, axis=1)
    grad_input = d_middle + norm_back(d_hidden_one * (1.0 + scale_one), normed_one, rscale_one)
    d_partial = jnp.concatenate(
        [d_shift_one, d_scale_one, d_gate_one, d_shift_two, d_scale_two, d_gate_two], axis=-1
    )
    d_modulation = lax.psum(d_partial, "seq").astype(jnp.bfloat16)
    d_lifted = jnp.einsum("be,ce->bc", d_modulation, ada_w, preferred_element_type=jnp.float32)
    grad_condition = silu_back(d_lifted)[0]
    grad_ada = jnp.einsum("bc,be->ce", lifted_b, d_modulation, preferred_element_type=jnp.float32)
    bias_ada = jnp.sum(d_modulation, axis=0, dtype=jnp.float32)
    total_ada, total_bada = (
        lax.psum_scatter(
            grad_ada.astype(jnp.bfloat16), "fsdp", scatter_dimension=0, tiled=True
        ).astype(jnp.float32),
        lax.psum_scatter(
            bias_ada.astype(jnp.bfloat16), "fsdp", scatter_dimension=0, tiled=True
        ).astype(jnp.float32),
    )
    shard_qkv, shard_bqv, shard_proj, shard_bproj, shard_fc1, shard_bfc1, shard_fc2, shard_bfc2 = (
        lax.psum_scatter(grad_qkv, "fsdp", scatter_dimension=0, tiled=True),
        lax.psum_scatter(bias_qv, "fsdp", scatter_dimension=0, tiled=True),
        lax.psum_scatter(grad_proj, "fsdp", scatter_dimension=0, tiled=True),
        lax.psum_scatter(bias_proj, "fsdp", scatter_dimension=0, tiled=True),
        lax.psum_scatter(grad_fc1, "fsdp", scatter_dimension=0, tiled=True),
        lax.psum_scatter(bias_fc1, "fsdp", scatter_dimension=0, tiled=True),
        lax.psum_scatter(grad_fc2, "fsdp", scatter_dimension=0, tiled=True),
        lax.psum_scatter(bias_fc2, "fsdp", scatter_dimension=0, tiled=True),
    )
    total_qkv, total_bqv, total_proj, total_bproj, total_fc1, total_bfc1, total_fc2, total_bfc2 = (
        lax.psum(
            (
                shard_qkv,
                shard_bqv,
                shard_proj,
                shard_bproj,
                shard_fc1,
                shard_bfc1,
                shard_fc2,
                shard_bfc2,
            ),
            "seq",
        )
    )
    return (
        result,
        grad_input,
        grad_condition,
        total_ada,
        total_bada,
        total_qkv,
        total_bqv,
        total_proj,
        total_bproj,
        total_fc1,
        total_bfc1,
        total_fc2,
        total_bfc2,
    )


def solution(mesh):
    return jax.shard_map(
        on_device,
        mesh=mesh,
        in_specs=(
            P("fsdp", "seq", None),
            P("fsdp", None),
            P("fsdp", None),
            P("fsdp"),
            P("fsdp", None),
            P("fsdp"),
            P("fsdp", None),
            P("fsdp"),
            P("fsdp", None),
            P("fsdp"),
            P("fsdp", None),
            P("fsdp"),
            P("fsdp", "seq", None),
        ),
        out_specs=(
            P("fsdp", "seq", None),
            P("fsdp", "seq", None),
            P("fsdp", None),
            P("fsdp", None),
            P("fsdp"),
            P("fsdp", None),
            P("fsdp"),
            P("fsdp", None),
            P("fsdp"),
            P("fsdp", None),
            P("fsdp"),
            P("fsdp", None),
            P("fsdp"),
        ),
        check_vma=False,
    )
```

profile of v0, /device:TPU:0, one launch (start us, length us, event | category | flops | bytes accessed | tf_op | source)
XLA Modules:
  0.0 1429.1 jit_solution(12914743900525769951)
XLA Ops:
  12.0 23.8 %all-gather.1 = bf16[16,1,128]{2,1,0:T(2,128)(2,1)S(1)} all-gather(bf16[1,1,128]{2,1,0:T(2,128)(2,1)} %bitcast.251), channel_id=1, replica_groups=mesh['fsdp'=16,'seq'=2] {'fsdp'}, dimensions={0}, use_global_device_ids=true | all-gather | bytes 4352 | tf_op jit(solution)/shard_map/all_gather | solution.py:107
  36.5 18.1 %all-gather = bf16[16,1,384]{2,1,0:T(2,128)(2,1)S(1)} all-gather(bf16[1,1,384]{2,1,0:T(2,128)(2,1)S(1)} %reshape.506), channel_id=1, replica_groups=mesh['fsdp'=16,'seq'=2] {'fsdp'}, dimensions={0}, use_global_device_ids=true | all-gather | bytes 13056 | tf_op jit(solution)/shard_map/all_gather | solution.py:105
  56.7 56.9 %all-gather.9.cloned.1.call-done = bf16[1024,6144]{1,0:T(8,128)(2,1)} async-done(((bf16[64,6144]{1,0:T(8,128)(2,1)}), bf16[1024,6144]{1,0:T(8,128)(2,1)}) %all-gather.9.cloned.1.call-update) | async-done | bytes 12582928 | tf_op jit(solution)/shard_map/all_gather | solution.py:104
  113.6 6.3 fusion.96
  120.0 55.6 %all-gather.11.cloned.1.call-done = bf16[1024,3072]{1,0:T(8,128)(2,1)} async-done(((bf16[64,3072]{1,0:T(8,128)(2,1)}), bf16[1024,3072]{1,0:T(8,128)(2,1)}) %all-gather.11.cloned.1.call-update) | async-done | bytes 6291472 | tf_op jit(solution)/shard_map/all_gather | solution.py:106
  175.6 7.8 add_convert_fusion
  183.4 7.1 reshape.484
  191.0 39.7 %all_to_all.63 = bf16[1,512,3,2,512]{4,1,2,0,3:T(8,128)(2,1)S(1)} all-to-all(bf16[1,512,3,2,512]{4,1,2,0,3:T(8,128)(2,1)S(1)} %copy.46), channel_id=1, replica_groups=mesh['fsdp'=16,'seq'=2] {'seq'}, dimensions={3} | all-to-all | bytes 6291456 | tf_op jit(solution)/shard_map/all_to_all | solution.py:132
  237.3 8.6 multiply_reduce_fusion.3
  249.4 5.6 copy-done.1
  262.9 7.8 fusion.72
  275.9 9.0 reduce.38
  287.5 4.5 all-to-all-start.1
  293.8 30.7 %all-reduce.10 = (bf16[1024]{0:T(1024)(128)(2,1)S(1)}, bf16[1024]{0:T(1024)(128)(2,1)S(1)}) all-reduce(bf16[1024]{0:T(1024)(128)(2,1)S(1)} %dynamic-update-slice, bf16[1024]{0:T(1024)(128)(2,1)S(1)} %dynamic-update-slice.1), channel_id=1, replica_groups=mesh['fsdp'=16,'seq'=2] {'fsdp'}, use_global_device_ids=true, to_apply=%add | all-reduce | flops 2048 | bytes 8192
  324.5 17.6 %all-gather.2 = bf16[16,1,256]{2,1,0:T(2,128)(2,1)S(1)} all-gather(bf16[1,1,256]{2,1,0:T(2,128)(2,1)S(1)} %reshape.510), channel_id=1, replica_groups=mesh['fsdp'=16,'seq'=2] {'fsdp'}, dimensions={0}, use_global_device_ids=true | all-gather | bytes 8704 | tf_op jit(solution)/shard_map/all_gather | solution.py:111
  350.3 4.6 fusion.127
  356.6 12.0 fusion.122
  368.6 13.9 convert_reduce_fusion
  382.5 9.8 fusion.55
  393.1 10.4 convert_reduce_fusion.3
  413.4 4.9 fusion.76
  418.4 9.5 all-to-all-done.2
  432.2 8.2 fusion.29
  440.4 8.7 add_convert_fusion.1
  449.1 5.9 copy.58
  455.0 8.1 fusion.90
  463.1 37.1 %fusion.64 = bf16[8,64,512]{2,1,0:T(8,128)(2,1)} fusion(bf16[1024,8,64]{0,2,1:T(8,128)(2,1)S(1)} %bitcast.199, f32[8,512,1024]{2,1,0:T(8,128)} %fusion.90, f32[8,512]{1,0:T(8,128)S(1)} %log_add_fusion, f32[8,512,1024]{2,1,0:T(8,128)} %copy-done), kind=kOutput, calls=%fused_computation.90 | convolution fusion | flops 574886912 | bytes 35143680 | tf_op jit(solution)/shard_map/bhqk,bkhd->bqhd/dot_general | solution.py:74
  503.7 8.1 fusion.89
  511.8 36.6 %fusion.67 = bf16[8,64,512]{2,1,0:T(8,128)(2,1)S(1)} fusion(bf16[1024,8,64]{0,2,1:T(8,128)(2,1)S(1)} %bitcast.200, f32[8,512,1024]{2,1,0:T(8,128)} %fusion.89, f32[8,512]{1,0:T(8,128)S(1)} %log_add_fusion.1, f32[8,512,1024]{2,1,0:T(8,128)} %get-tuple-element.67), kind=kOutput, calls=%fused_computation.91 | convolution fusion | flops 574886912 | bytes 35143680 | tf_op jit(solution)/shard_map/bhqk,bkhd->bqhd/dot_general | solution.py:74
  550.4 30.7 %fusion.11 = f32[8,64,1024]{2,1,0:T(8,128)} fusion(f32[8,512,1024]{2,1,0:T(8,128)} %fusion.89, f32[8,512,1024]{2,1,0:T(8,128)} %get-tuple-element.67, f32[8,512]{1,0:T(8,128)S(1)} %log_add_fusion.1, bf16[1,1024,8,64]{1,3,2,0:T(8,128)(2,1)S(1)} %bitcast.210), kind=kOutput, calls=%fused_computation.21 | convolution fusion | flops 574624768 | bytes 69763072 | tf_op jit(solution)/shard_map/bhqk,bqhd->bkhd/dot_general | solution.py:76
  581.1 31.5 %add_convert_fusion.2 = bf16[8,64,1024]{2,1,0:T(8,128)(2,1)} fusion(f32[8,64,1024]{2,1,0:T(8,128)} %fusion.11, f32[8,512,1024]{2,1,0:T(8,128)} %fusion.90, f32[8,512]{1,0:T(8,128)S(1)} %log_add_fusion, f32[8,512,1024]{2,1,0:T(8,128)} %copy-done, bf16[1,1024,8,64]{1,3,2,0:T(8,128)(2,1)} %bitcast.208), kind=kOutput, calls=%fused_computation.82 | convolution fusion | flops 575673344 | bytes 70811648 | tf_op jit(solution)/shard_map/bhqk,bqhd->bkhd/dot_general | solution.py:76
  612.6 5.9 copy.57
  618.5 8.6 pad_maximum_fusion
  627.1 50.3 %all_to_all.64 = bf16[1,1024,3,1,512]{4,2,3,0,1:T(4,128)(2,1)S(1)} all-to-all(bf16[1,1024,3,1,512]{4,2,3,0,1:T(4,128)(2,1)S(1)} %pad_maximum_fusion), channel_id=1, replica_groups=mesh['fsdp'=16,'seq'=2] {'seq'}, dimensions={1} | all-to-all | bytes 6291456 | tf_op jit(solution)/shard_map/all_to_all | solution.py:197
  681.1 10.5 fusion.117
  691.7 18.5 %fusion.79 = f32[4096,1024]{1,0:T(8,128)} fusion(bf16[1,512,1024]{2,1,0:T(8,128)(2,1)} %param.25, f32[1024]{0:T(1024)S(1)} %bitcast.243, f32[512,4096]{1,0:T(8,128)} %fusion.122, f32[4096]{0:T(1024)S(1)} %bitcast.236), kind=kOutput, calls=%fused_computation.102 | convolution fusion | flops 4317511680 | bytes 26234880 | tf_op jit(solution)/shard_map/btf,btd->fd/dot_general | solution.py:168
  710.8 15.0 %fusion.120 = f32[1024,4096]{1,0:T(8,128)} fusion(bf16[512,4096]{1,0:T(8,128)(2,1)} %copy-done.37, f32[1,512,1024]{2,1,0:T(8,128)} %copy-done.9, f32[1024]{0:T(1024)S(1)} %bitcast.240, f32[1024]{0:T(1024)S(1)} %bitcast.230, f32[512]{0:T(512)S(1)} %add_rsqrt_fusion, f32[512]{0:T(512)S(1)} %broadcast_multiply_fusion.4), kind=kOutput, calls=%fused_computation.165 | convolution fusion | flops 4297588736 | bytes 23080960 | tf_op jit(solution)/shard_map/btd,btf->df/dot_general | solution.py:172
  728.3 61.3 %all-reduce.7 = (f32[2048]{0:T(1024)S(1)}, f32[1024]{0:T(1024)S(1)}, f32[4096]{0:T(1024)S(1)}, f32[1024]{0:T(1024)S(1)}) all-reduce(f32[2048]{0:T(1024)S(1)} %pad_maximum_fusion.2, f32[1024]{0:T(1024)S(1)} %get-tuple-element.47, f32[4096]{0:T(1024)S(1)} %copy-done.21, ...), channel_id=5, replica_groups=mesh['fsdp'=16,'seq'=2] {'fsdp'}, use_global_device_ids=true, to_apply=%region_26.27.clone | all-reduce | flops 8192 | bytes 65536
  789.9 8.1 fusion.51
  800.8 9.9 all-reduce.8
  810.8 7.4 multiply_convert_fusion
  818.3 8.7 reduce-scatter.8.cloned.1.call-done
  827.0 180.7 %reduce-scatter.14.cloned.1.call-done = f32[256,1024]{1,0:T(8,128)} async-done(((f32[4096,1024]{1,0:T(8,128)}), f32[256,1024]{1,0:T(8,128)}) %reduce-scatter.14.cloned.1.call-update) | async-done | bytes 1048592 | tf_op jit(solution)/shard_map/reduce_scatter | solution.py:230
  1007.7 180.6 %reduce-scatter.12.cloned.1.call-done = f32[64,4096]{1,0:T(8,128)} async-done(((f32[1024,4096]{1,0:T(8,128)}), f32[64,4096]{1,0:T(8,128)}) %reduce-scatter.12.cloned.1.call-update) | async-done | bytes 1048592 | tf_op jit(solution)/shard_map/reduce_scatter | solution.py:228
  1188.9 61.3 %all-reduce.2 = bf16[6144]{0:T(1024)(128)(2,1)S(1)} all-reduce(bf16[6144]{0:T(1024)(128)(2,1)S(1)} %convert_reduce_fusion.5), channel_id=3, replica_groups=mesh['fsdp'=16,'seq'=2] {'fsdp'}, use_global_device_ids=true, to_apply=%region_22.23.clone | all-reduce | flops 6144 | bytes 24576
  1250.8 8.7 fusion.95
  1259.5 67.0 %reduce-scatter.6.cloned.1.call-done = bf16[64,6144]{1,0:T(8,128)(2,1)} async-done(((bf16[1024,6144]{1,0:T(8,128)(2,1)}), bf16[64,6144]{1,0:T(8,128)(2,1)}) %reduce-scatter.6.cloned.1.call-update) | async-done | bytes 786448 | tf_op jit(solution)/shard_map/reduce_scatter | solution.py:216
  1328.8 85.2 %all-reduce.13.cloned.1.call-done = (f32[64,3072]{1,0:T(8,128)}, f32[64,1024]{1,0:T(8,128)}, f32[64,4096]{1,0:T(8,128)}, f32[256,1024]{1,0:T(8,128)}) async-done(((f32[64,3072]{1,0:T(8,128)}, f32[64,1024]{1,0:T(8,128)}, f32[64,4096]{1,0:T(8,128)}, f32[256,1024]{1,0:T(8,128)}), (f32[64,3072]{1,0:T(8,128)}, f32[64,1024]{1,0:T(8,128)}, f32[64,4096]{1,0:T(8,128)}, ...) | async-done | bytes 3145744 | tf_op jit(solution)/shard_map/psum | solution.py:234
  (187 shorter events, 84.7 us)
Async XLA Ops:
  7.2 106.4 %all-gather.9.cloned.1.call-start = ((), (), s32[]{:S(2)}) async-start(), calls=%async_computation.9 | async-start | bytes 13369344 | tf_op jit(solution)/shard_map/all_gather | solution.py:104
  7.9 167.6 %all-gather.11.cloned.1.call-start = ((), (), s32[]{:S(2)}) async-start(), calls=%async_computation.10 | async-start | bytes 6684672 | tf_op jit(solution)/shard_map/all_gather | solution.py:106
  8.7 341.7 %all-gather.13.cloned.1.call-start = ((), (), s32[]{:S(2)}) async-start(), calls=%async_computation.11 | async-start | bytes 2228224 | tf_op jit(solution)/shard_map/all_gather | solution.py:108
  9.4 347.2 %all-gather.15.cloned.1.call-start = ((), (), s32[]{:S(2)}) async-start(), calls=%async_computation.12 | async-start | bytes 8912896 | tf_op jit(solution)/shard_map/all_gather | solution.py:110
  10.0 358.7 %all-gather.17.cloned.1.call-start = ((), (), s32[]{:S(2)}) async-start(), calls=%async_computation.13 | async-start | bytes 8912896 | tf_op jit(solution)/shard_map/all_gather | solution.py:112
  54.7 120.8 %copy-start.16 = (f32[512]{0:T(512)}, f32[512]{0:T(512)S(1)}, u32[]{:S(2)}) copy-start(f32[512]{0:T(512)S(1)} %broadcast_multiply_fusion.5) | copy-start | bytes 6148
  56.7 118.9 %copy-start.22 = (f32[512]{0:T(512)}, f32[512]{0:T(512)S(1)}, u32[]{:S(2)}) copy-start(f32[512]{0:T(512)S(1)} %add_rsqrt_fusion.1) | copy-start | bytes 6148
  56.7 118.9 %copy-start.2 = (bf16[1,512,1024]{2,1,0:T(8,128)(2,1)S(1)}, bf16[1,512,1024]{2,1,0:T(8,128)(2,1)}, u32[]{:S(2)}) copy-start(bf16[1,512,1024]{2,1,0:T(8,128)(2,1)} %param.13) | copy-start | bytes 3145732
  119.9 55.6 %copy-start.14 = (f32[1,1,1024]{2,1,0:T(1,128)}, f32[1,1,1024]{2,1,0:T(1,128)S(1)}, u32[]{:S(2)}) copy-start(f32[1,1,1024]{2,1,0:T(1,128)S(1)} %get-tuple-element.56) | copy-start | bytes 12292
  120.0 55.6 %copy-start.26 = (f32[1,1,1024]{2,1,0:T(1,128)}, f32[1,1,1024]{2,1,0:T(1,128)S(1)}, u32[]{:S(2)}) copy-start(f32[1,1,1024]{2,1,0:T(1,128)S(1)} %get-tuple-element.55) | copy-start | bytes 12292
  120.0 236.6 %copy-start.24 = (f32[1,1,1024]{2,1,0:T(1,128)}, f32[1,1,1024]{2,1,0:T(1,128)S(1)}, u32[]{:S(2)}) copy-start(f32[1,1,1024]{2,1,0:T(1,128)S(1)} %get-tuple-element.53) | copy-start | bytes 12292
  233.7 3.6 copy-start.7
  237.3 21.3 %copy-start = (f32[8,512,1024]{2,1,0:T(8,128)}, f32[8,512,1024]{2,1,0:T(8,128)S(1)}, u32[]{:S(2)}) copy-start(f32[8,512,1024]{2,1,0:T(8,128)S(1)} %get-tuple-element.65) | copy-start | bytes 50331652
  245.9 9.1 copy-start.1
  270.8 21.2 %copy-start.33 = (bf16[256]{0:T(256)(128)(2,1)S(1)}, bf16[256]{0:T(256)(128)(2,1)}, u32[]{:S(2)}) copy-start(bf16[256]{0:T(256)(128)(2,1)} %param.22) | copy-start | bytes 1540
  270.8 21.3 %copy-start.29 = (u32[32]{0:T(128)S(1)}, u32[32]{0:T(128)}, u32[]{:S(2)}) copy-start(u32[32]{0:T(128)} %constant.40) | copy-start | bytes 388
  270.8 22.5 %copy-start.34 = (bf16[64]{0:T(256)(128)(2,1)S(1)}, bf16[64]{0:T(256)(128)(2,1)}, u32[]{:S(2)}) copy-start(bf16[64]{0:T(256)(128)(2,1)} %param.24) | copy-start | bytes 388
  270.8 22.8 %copy-start.35 = (bf16[64]{0:T(256)(128)(2,1)S(1)}, bf16[64]{0:T(256)(128)(2,1)}, u32[]{:S(2)}) copy-start(bf16[64]{0:T(256)(128)(2,1)} %param.20) | copy-start | bytes 388
  275.3 75.0 %copy-start.3 = (bf16[1,512,1024]{2,1,0:T(8,128)(2,1)S(1)}, bf16[1,512,1024]{2,1,0:T(8,128)(2,1)}, u32[]{:S(2)}) copy-start(bf16[1,512,1024]{2,1,0:T(8,128)(2,1)} %param.13) | copy-start | bytes 3145732
  287.5 54.6 %all-to-all-start.1 = ((bf16[2,2,131072]{2,1,0:T(2,128)(2,1)}), bf16[2,2,131072]{2,1,0:T(2,128)(2,1)}, u32[]{:S(2)}, u32[]{:S(2)}) async-start(bf16[2,2,131072]{2,1,0:T(2,128)(2,1)} %reshape.533), calls=%async_computation.1 | async-start | bytes 2097152 | tf_op jit(solution)/shard_map/all_to_all | solution.py:144
  324.5 30.5 %copy-start.18 = (f32[1024]{0:T(1024)}, f32[1024]{0:T(1024)S(1)}, u32[]{:S(2)}) copy-start(f32[1024]{0:T(1024)S(1)} %convert_element_type.179) | copy-start | bytes 12292
  356.6 12.0 copy-start.32
  368.6 13.9 copy-start.10
  382.5 9.8 copy-start.37
  382.5 10.6 copy-start.30
  393.1 11.4 copy-start.31
  409.8 18.1 %all-to-all-start.2 = ((bf16[1,512,2,512]{3,1,0,2:T(8,128)(2,1)}), bf16[1,512,2,512]{3,1,0,2:T(8,128)(2,1)S(1)}, u32[]{:S(2)}, u32[]{:S(2)}) async-start(bf16[1,512,2,512]{3,1,0,2:T(8,128)(2,1)} %copy.53), calls=%async_computation.2 | async-start | bytes 2097152 | tf_op jit(solution)/shard_map/all_to_all | solution.py:185
  413.3 404.9 %reduce-scatter.10.cloned.1.call-start = ((), (), s32[]{:S(2)}) async-start(), calls=%async_computation.16 | async-start | bytes 4456448 | tf_op jit(solution)/shard_map/reduce_scatter | solution.py:226
  418.4 408.6 %reduce-scatter.8.cloned.1.call-start = ((), (), s32[]{:S(2)}) async-start(), calls=%async_computation.15 | async-start | bytes 13369344 | tf_op jit(solution)/shard_map/reduce_scatter | solution.py:224
  511.8 38.6 %copy-start.8 = (bf16[1,1024,1,1,512]{1,4,3,2,0:T(8,128)(2,1)S(1)}, bf16[1,1024,1,1,512]{1,4,3,2,0:T(8,128)(2,1)}, u32[]{:S(2)}) copy-start(bf16[1,1024,1,1,512]{1,4,3,2,0:T(8,128)(2,1)} %copy.49) | copy-start | bytes 3145732
  581.1 37.5 %copy-start.5 = (bf16[1,1024,1,1,512]{4,2,3,0,1:T(2,128)(2,1)S(1)}, bf16[1,1024,1,1,512]{4,2,3,0,1:T(2,128)(2,1)}, u32[]{:S(2)}) copy-start(bf16[1,1024,1,1,512]{4,2,3,0,1:T(2,128)(2,1)} %copy.58) | copy-start | bytes 3145732
  581.1 37.5 %copy-start.6 = (bf16[1,512,1,1,512]{4,2,3,0,1:T(2,128)(2,1)S(1)}, bf16[1,512,1,1,512]{4,2,3,0,1:T(2,128)(2,1)}, u32[]{:S(2)}) copy-start(bf16[1,512,1,1,512]{4,2,3,0,1:T(2,128)(2,1)} %copy.56) | copy-start | bytes 1572868
  677.5 3.6 copy-start.15
  677.5 3.6 copy-start.17
  677.5 3.6 copy-start.23
  677.5 3.6 copy-start.27
  691.6 316.1 %reduce-scatter.14.cloned.1.call-start = ((), (), s32[]{:S(2)}) async-start(), calls=%async_computation.18 | async-start | bytes 17825792 | tf_op jit(solution)/shard_map/reduce_scatter | solution.py:230
  710.2 478.1 %reduce-scatter.12.cloned.1.call-start = ((), (), s32[]{:S(2)}) async-start(), calls=%async_computation.17 | async-start | bytes 17825792 | tf_op jit(solution)/shard_map/reduce_scatter | solution.py:228
  725.9 1.9 copy-start.13
  725.9 2.4 copy-start.21
  725.9 600.6 %reduce-scatter.6.cloned.1.call-start = ((), (), s32[]{:S(2)}) async-start(), calls=%async_computation.14 | async-start | bytes 13369344 | tf_op jit(solution)/shard_map/reduce_scatter | solution.py:216
  789.9 8.5 copy-start.4
  789.9 8.5 copy-start.11
  789.9 8.5 copy-start.12
  789.9 8.5 copy-start.19
  798.0 2.7 copy-start.20
  798.0 2.7 copy-start.28
  818.2 595.9 %all-reduce.13.cloned.1.call-start = ((), (), s32[]{:S(2)}) async-start(), calls=%async_computation.19 | async-start | bytes 6291456 | tf_op jit(solution)/shard_map/psum | solution.py:234
  (3 other events, 3.0 us)
Sparse Core Ops, SparseCore 0:
  10.3 103.2 all-gather.8
  115.9 59.6 all-gather.10
  177.7 40.1 all-gather.12
  219.9 73.0 all-gather.14
  295.0 73.1 all-gather.16
  418.5 72.8 reduce-scatter.9
  691.7 135.2 reduce-scatter.7
  831.1 176.5 reduce-scatter.13
  1011.9 176.4 reduce-scatter.11
  1192.2 134.2 reduce-scatter.5
  1328.9 85.0 all-reduce.12
where the time goes:
time: 1440 us; the launch traced here: 1430 us
  waiting for transfers between devices  647 us (45%)
  matrix products  326 us (23%)
  blocking collectives  313 us (22%)
  local copies, waits for them, and re-layouts  73.4 us (5%)
  other arithmetic  42.9 us (3%)
  between operations  17.8 us (1%)
    reduce_scatter x1, waiting for transfers between devices, on_device(): lax.psum_scatter(grad_fc2, 'fsdp', scatter_dimension=0, tiled=True)  181 us
    reduce_scatter x1, waiting for transfers between devices, on_device(): lax.psum_scatter(grad_fc1, 'fsdp', scatter_dimension=0, tiled=True)  181 us
    unnamed x3, blocking collectives  153 us
    psum x1, waiting for transfers between devices, on_device(): lax.psum((shard_qkv, shard_bqv, shard_proj, shard_bproj, shard_fc1, shard...  85.2 us
    dot_general x2, matrix products, attend_backward(): jnp.einsum('bhqk,bkhd->bqhd', d_raw, keys_all, preferred_element_type=jnp...  73.6 us
    reduce_scatter x1, waiting for transfers between devices, on_device(): lax.psum_scatter(grad_ada.astype(jnp.bfloat16), 'fsdp', scatter_dimension...  67 us
    dot_general x2, matrix products, attend_backward(): jnp.einsum('bhqk,bqhd->bkhd', d_raw, q_block, preferred_element_type=jnp....  62.2 us
    all_gather x1, waiting for transfers between devices, on_device(): lax.all_gather(w_ada, 'fsdp', axis=0, tiled=True)  56.9 us
  transfers between devices with their start and end apart: 13, of which 8 were waited for; matrix products, arithmetic and copies ran while one was open for 27% of the time, Pallas kernels for 0%

commit v1 on v0

--- a/solution.py
+++ b/solution.py
@@ -194,9 +194,10 @@
     d_spread = jnp.stack([grad_q, grad_k, grad_v], axis=2).reshape(
         latents, seq_len, 3, 1, group_width
     )
-    d_qkv = lax.all_to_all(d_spread, "seq", split_axis=1, concat_axis=3, tiled=True).reshape(
-        latents, local_len, 3 * model_width
-    )
+    d_qkv = jnp.concatenate(
+        lax.all_to_all(jnp.stack(jnp.split(d_spread, lax.axis_size("seq"), axis=1)), "seq", 0, 0),
+        axis=3,
+    ).reshape(latents, local_len, 3 * model_width)
     grad_qkv = jnp.einsum("btd,bte->de", hidden_one, d_qkv, preferred_element_type=jnp.float32)
     column_sums = jnp.sum(d_qkv, axis=(0, 1), dtype=jnp.float32)
     bias_qv = jnp.concatenate([column_sums[:model_width], column_sums[2 * model_width :]])

time: 1440 us -> 1390 us (0.965)
  local copies, waits for them, and re-layouts: 73.4 us -> 54.9 us
    unnamed x101 -> x99, local copies, waits for them, and re-layouts: 27.8 us -> 29.8 us
  transfers between devices with their start and end apart: 13 -> 13, of which waited for: 8 -> 8; matrix products, arithmetic and copies ran while one was open for 27% -> 25% of each run, Pallas kernels for 0% -> 0%
where the time goes in v1:
time: 1390 us; the launch traced here: 1380 us
  waiting for transfers between devices  646 us (46%)
  matrix products  320 us (23%)
  blocking collectives  302 us (22%)
  local copies, waits for them, and re-layouts  54.9 us (4%)
  other arithmetic  34.5 us (2%)
  between operations  18 us (1%)
    reduce_scatter x1, waiting for transfers between devices, on_device(): lax.psum_scatter(grad_fc2, 'fsdp', scatter_dimension=0, tiled=True)  181 us
    reduce_scatter x1, waiting for transfers between devices, on_device(): lax.psum_scatter(grad_fc1, 'fsdp', scatter_dimension=0, tiled=True)  181 us
    unnamed x3, blocking collectives  154 us
    psum x1, waiting for transfers between devices, on_device(): lax.psum((shard_qkv, shard_bqv, shard_proj, shard_bproj, shard_fc1, shard...  85.2 us
    dot_general x2, matrix products, attend_backward(): jnp.einsum('bhqk,bkhd->bqhd', d_raw, keys_all, preferred_element_type=jnp...  74.1 us
    reduce_scatter x1, waiting for transfers between devices, on_device(): lax.psum_scatter(grad_ada.astype(jnp.bfloat16), 'fsdp', scatter_dimension...  66.4 us
    dot_general x2, matrix products, attend_backward(): jnp.einsum('bhqk,bqhd->bkhd', d_raw, q_block, preferred_element_type=jnp....  60.7 us
    all_gather x1, waiting for transfers between devices, on_device(): lax.all_gather(w_ada, 'fsdp', axis=0, tiled=True)  56.9 us
  transfers between devices with their start and end apart: 13, of which 8 were waited for; matrix products, arithmetic and copies ran while one was open for 25% of the time, Pallas kernels for 0%

profile of v1, /device:TPU:0, one launch (start us, length us, event | category | flops | bytes accessed | tf_op | source)
XLA Modules:
  0.0 1383.5 jit_solution(2176841012532353997)
XLA Ops:
  12.0 23.8 %all-gather.1 = bf16[16,1,128]{2,1,0:T(2,128)(2,1)S(1)} all-gather(bf16[1,1,128]{2,1,0:T(2,128)(2,1)} %bitcast.261), channel_id=1, replica_groups=mesh['fsdp'=16,'seq'=2] {'fsdp'}, dimensions={0}, use_global_device_ids=true | all-gather | bytes 4352 | tf_op jit(solution)/shard_map/all_gather | solution.py:107
  36.5 18.1 %all-gather = bf16[16,1,384]{2,1,0:T(2,128)(2,1)S(1)} all-gather(bf16[1,1,384]{2,1,0:T(2,128)(2,1)S(1)} %reshape.508), channel_id=1, replica_groups=mesh['fsdp'=16,'seq'=2] {'fsdp'}, dimensions={0}, use_global_device_ids=true | all-gather | bytes 13056 | tf_op jit(solution)/shard_map/all_gather | solution.py:105
  56.7 56.9 %all-gather.9.cloned.1.call-done = bf16[1024,6144]{1,0:T(8,128)(2,1)} async-done(((bf16[64,6144]{1,0:T(8,128)(2,1)}), bf16[1024,6144]{1,0:T(8,128)(2,1)}) %all-gather.9.cloned.1.call-update) | async-done | bytes 12582928 | tf_op jit(solution)/shard_map/all_gather | solution.py:104
  113.6 6.3 fusion.96
  120.0 55.6 %all-gather.11.cloned.1.call-done = bf16[1024,3072]{1,0:T(8,128)(2,1)} async-done(((bf16[64,3072]{1,0:T(8,128)(2,1)}), bf16[1024,3072]{1,0:T(8,128)(2,1)}) %all-gather.11.cloned.1.call-update) | async-done | bytes 6291472 | tf_op jit(solution)/shard_map/all_gather | solution.py:106
  175.6 7.8 add_convert_fusion
  183.4 7.1 reshape.485
  191.0 39.6 %all_to_all.53 = bf16[1,512,3,2,512]{4,1,2,0,3:T(8,128)(2,1)S(1)} all-to-all(bf16[1,512,3,2,512]{4,1,2,0,3:T(8,128)(2,1)S(1)} %copy.52), channel_id=1, replica_groups=mesh['fsdp'=16,'seq'=2] {'seq'}, dimensions={3} | all-to-all | bytes 6291456 | tf_op jit(solution)/shard_map/all_to_all | solution.py:132
  233.6 3.6 multiply_reduce_fusion.2
  237.2 8.6 multiply_reduce_fusion.3
  249.3 5.6 copy-done.1
  258.5 4.3 fusion.73
  262.9 7.8 fusion.72
  270.9 4.3 copy.57
  275.7 9.0 reduce.38
  287.3 4.5 all-to-all-start.1
  293.5 30.6 %all-reduce.10 = (bf16[1024]{0:T(1024)(128)(2,1)S(1)}, bf16[1024]{0:T(1024)(128)(2,1)S(1)}) all-reduce(bf16[1024]{0:T(1024)(128)(2,1)S(1)} %dynamic-update-slice, bf16[1024]{0:T(1024)(128)(2,1)S(1)} %dynamic-update-slice.1), channel_id=1, replica_groups=mesh['fsdp'=16,'seq'=2] {'fsdp'}, use_global_device_ids=true, to_apply=%add | all-reduce | flops 2048 | bytes 8192
  324.1 17.7 %all-gather.2 = bf16[16,1,256]{2,1,0:T(2,128)(2,1)S(1)} all-gather(bf16[1,1,256]{2,1,0:T(2,128)(2,1)S(1)} %reshape.512), channel_id=1, replica_groups=mesh['fsdp'=16,'seq'=2] {'fsdp'}, dimensions={0}, use_global_device_ids=true | all-gather | bytes 8704 | tf_op jit(solution)/shard_map/all_gather | solution.py:111
  350.1 4.6 fusion.127
  356.4 12.0 fusion.122
  368.4 13.3 convert_reduce_fusion
  381.7 9.6 fusion.55
  391.7 10.5 convert_reduce_fusion.3
  412.1 4.9 fusion.76
  417.1 9.6 all-to-all-done.2
  431.0 8.4 fusion.90
  439.5 8.5 fusion.89
  447.9 37.1 %fusion.64 = bf16[8,64,512]{2,1,0:T(8,128)(2,1)} fusion(bf16[1024,8,64]{0,2,1:T(8,128)(2,1)S(1)} %bitcast.209, f32[8,512,1024]{2,1,0:T(8,128)} %fusion.90, f32[8,512]{1,0:T(8,128)S(1)} %log_add_fusion, f32[8,512,1024]{2,1,0:T(8,128)} %copy-done), kind=kOutput, calls=%fused_computation.93 | convolution fusion | flops 574886912 | bytes 35143680 | tf_op jit(solution)/shard_map/bhqk,bkhd->bqhd/dot_general | solution.py:74
  485.0 37.1 %fusion.67 = bf16[8,64,512]{2,1,0:T(8,128)(2,1)} fusion(bf16[1024,8,64]{0,2,1:T(8,128)(2,1)S(1)} %bitcast.210, f32[8,512,1024]{2,1,0:T(8,128)} %fusion.89, f32[8,512]{1,0:T(8,128)S(1)} %log_add_fusion.1, f32[8,512,1024]{2,1,0:T(8,128)} %get-tuple-element.69), kind=kOutput, calls=%fused_computation.94 | convolution fusion | flops 574886912 | bytes 35143680 | tf_op jit(solution)/shard_map/bhqk,bkhd->bqhd/dot_general | solution.py:74
  522.1 30.9 %fusion.11 = f32[8,64,1024]{2,1,0:T(8,128)} fusion(f32[8,512,1024]{2,1,0:T(8,128)} %fusion.89, f32[8,512,1024]{2,1,0:T(8,128)} %get-tuple-element.69, f32[8,512]{1,0:T(8,128)S(1)} %log_add_fusion.1, bf16[1,1024,8,64]{1,3,2,0:T(8,128)(2,1)S(1)} %bitcast.219), kind=kOutput, calls=%fused_computation.21 | convolution fusion | flops 574624768 | bytes 69763072 | tf_op jit(solution)/shard_map/bhqk,bqhd->bkhd/dot_general | solution.py:76
  552.9 29.8 %add_convert_fusion.2 = bf16[8,64,1024]{2,1,0:T(8,128)(2,1)S(1)} fusion(f32[8,64,1024]{2,1,0:T(8,128)} %fusion.11, f32[8,512,1024]{2,1,0:T(8,128)} %fusion.90, f32[8,512]{1,0:T(8,128)S(1)} %log_add_fusion, f32[8,512,1024]{2,1,0:T(8,128)} %copy-done, bf16[1,1024,8,64]{1,3,2,0:T(8,128)(2,1)S(1)} %bitcast.220), kind=kOutput, calls=%fused_computation.83 | convolution fusion | flops 575673344 | bytes 70811648 | tf_op jit(solution)/shard_map/bhqk,bqhd->bkhd/dot_general | solution.py:76
  582.8 7.4 fusion.29
  590.2 7.8 add_convert_fusion.1
  599.0 39.0 %all_to_all.54 = bf16[2,1,512,3,1,512]{2,5,3,4,1,0:T(8,128)(2,1)S(1)} all-to-all(bf16[2,1,512,3,1,512]{2,5,3,4,1,0:T(8,128)(2,1)S(1)} %pad_maximum_fusion.1), channel_id=1, replica_groups=mesh['fsdp'=16,'seq'=2] {'seq'}, dimensions={0} | all-to-all | bytes 6291456 | tf_op jit(solution)/shard_map/all_to_all | solution.py:198
  640.1 6.9 fusion.117
  647.2 19.0 %fusion.79 = f32[4096,1024]{1,0:T(8,128)} fusion(bf16[1,512,1024]{2,1,0:T(8,128)(2,1)} %param.25, f32[1024]{0:T(1024)S(1)} %bitcast.253, f32[512,4096]{1,0:T(8,128)} %fusion.122, f32[4096]{0:T(1024)S(1)} %bitcast.246), kind=kOutput, calls=%fused_computation.105 | convolution fusion | flops 4317511680 | bytes 26234880 | tf_op jit(solution)/shard_map/btf,btd->fd/dot_general | solution.py:168
  666.9 14.9 %fusion.120 = f32[1024,4096]{1,0:T(8,128)} fusion(bf16[512,4096]{1,0:T(8,128)(2,1)} %copy-done.36, f32[1,512,1024]{2,1,0:T(8,128)} %copy-done.9, f32[1024]{0:T(1024)S(1)} %bitcast.250, f32[1024]{0:T(1024)S(1)} %bitcast.240, f32[512]{0:T(512)S(1)} %add_rsqrt_fusion, f32[512]{0:T(512)S(1)} %broadcast_multiply_fusion.4), kind=kOutput, calls=%fused_computation.168 | convolution fusion | flops 4297588736 | bytes 23080960 | tf_op jit(solution)/shard_map/btd,btf->df/dot_general | solution.py:172
  684.1 61.6 %all-reduce.7 = (f32[2048]{0:T(1024)S(1)}, f32[1024]{0:T(1024)S(1)}, f32[4096]{0:T(1024)S(1)}, f32[1024]{0:T(1024)S(1)}) all-reduce(f32[2048]{0:T(1024)S(1)} %pad_maximum_fusion.3, f32[1024]{0:T(1024)S(1)} %get-tuple-element.49, f32[4096]{0:T(1024)S(1)} %get-tuple-element.73, ...), channel_id=5, replica_groups=mesh['fsdp'=16,'seq'=2] {'fsdp'}, use_global_device_ids=true, to_apply=%region_26.27.clone | all-reduce | flops 8192 | bytes 65536
  746.0 8.1 fusion.51
  756.8 9.4 all-reduce.8
  766.4 7.4 multiply_convert_fusion
  773.9 7.2 reduce-scatter.8.cloned.1.call-done
  781.1 180.7 %reduce-scatter.14.cloned.1.call-done = f32[256,1024]{1,0:T(8,128)} async-done(((f32[4096,1024]{1,0:T(8,128)}), f32[256,1024]{1,0:T(8,128)}) %reduce-scatter.14.cloned.1.call-update) | async-done | bytes 1048592 | tf_op jit(solution)/shard_map/reduce_scatter | solution.py:231
  961.8 180.6 %reduce-scatter.12.cloned.1.call-done = f32[64,4096]{1,0:T(8,128)} async-done(((f32[1024,4096]{1,0:T(8,128)}), f32[64,4096]{1,0:T(8,128)}) %reduce-scatter.12.cloned.1.call-update) | async-done | bytes 1048592 | tf_op jit(solution)/shard_map/reduce_scatter | solution.py:229
  1142.9 61.8 %all-reduce.2 = bf16[6144]{0:T(1024)(128)(2,1)S(1)} all-reduce(bf16[6144]{0:T(1024)(128)(2,1)S(1)} %convert_reduce_fusion.5), channel_id=3, replica_groups=mesh['fsdp'=16,'seq'=2] {'fsdp'}, use_global_device_ids=true, to_apply=%region_22.23.clone | all-reduce | flops 6144 | bytes 24576
  1205.4 8.6 fusion.95
  1214.0 66.4 %reduce-scatter.6.cloned.1.call-done = bf16[64,6144]{1,0:T(8,128)(2,1)} async-done(((bf16[1024,6144]{1,0:T(8,128)(2,1)}), bf16[64,6144]{1,0:T(8,128)(2,1)}) %reduce-scatter.6.cloned.1.call-update) | async-done | bytes 786448 | tf_op jit(solution)/shard_map/reduce_scatter | solution.py:217
  1282.9 85.2 %all-reduce.13.cloned.1.call-done = (f32[64,3072]{1,0:T(8,128)}, f32[64,1024]{1,0:T(8,128)}, f32[64,4096]{1,0:T(8,128)}, f32[256,1024]{1,0:T(8,128)}) async-done(((f32[64,3072]{1,0:T(8,128)}, f32[64,1024]{1,0:T(8,128)}, f32[64,4096]{1,0:T(8,128)}, f32[256,1024]{1,0:T(8,128)}), (f32[64,3072]{1,0:T(8,128)}, f32[64,1024]{1,0:T(8,128)}, f32[64,4096]{1,0:T(8,128)}, ...) | async-done | bytes 3145744 | tf_op jit(solution)/shard_map/psum | solution.py:235
  (182 shorter events, 65.8 us)
Async XLA Ops:
  7.2 106.4 %all-gather.9.cloned.1.call-start = ((), (), s32[]{:S(2)}) async-start(), calls=%async_computation.9 | async-start | bytes 13369344 | tf_op jit(solution)/shard_map/all_gather | solution.py:104
  7.9 167.6 %all-gather.11.cloned.1.call-start = ((), (), s32[]{:S(2)}) async-start(), calls=%async_computation.10 | async-start | bytes 6684672 | tf_op jit(solution)/shard_map/all_gather | solution.py:106
  8.7 341.4 %all-gather.13.cloned.1.call-start = ((), (), s32[]{:S(2)}) async-start(), calls=%async_computation.11 | async-start | bytes 2228224 | tf_op jit(solution)/shard_map/all_gather | solution.py:108
  9.4 347.0 %all-gather.15.cloned.1.call-start = ((), (), s32[]{:S(2)}) async-start(), calls=%async_computation.12 | async-start | bytes 8912896 | tf_op jit(solution)/shard_map/all_gather | solution.py:110
  10.0 358.4 %all-gather.17.cloned.1.call-start = ((), (), s32[]{:S(2)}) async-start(), calls=%async_computation.13 | async-start | bytes 8912896 | tf_op jit(solution)/shard_map/all_gather | solution.py:112
  54.7 120.8 %copy-start.18 = (f32[512]{0:T(512)}, f32[512]{0:T(512)S(1)}, u32[]{:S(2)}) copy-start(f32[512]{0:T(512)S(1)} %broadcast_multiply_fusion.5) | copy-start | bytes 6148
  56.7 118.9 %copy-start.22 = (f32[512]{0:T(512)}, f32[512]{0:T(512)S(1)}, u32[]{:S(2)}) copy-start(f32[512]{0:T(512)S(1)} %add_rsqrt_fusion.1) | copy-start | bytes 6148
  56.7 118.9 %copy-start.2 = (bf16[1,512,1024]{2,1,0:T(8,128)(2,1)S(1)}, bf16[1,512,1024]{2,1,0:T(8,128)(2,1)}, u32[]{:S(2)}) copy-start(bf16[1,512,1024]{2,1,0:T(8,128)(2,1)} %param.13) | copy-start | bytes 3145732
  119.9 55.6 %copy-start.16 = (f32[1,1,1024]{2,1,0:T(1,128)}, f32[1,1,1024]{2,1,0:T(1,128)S(1)}, u32[]{:S(2)}) copy-start(f32[1,1,1024]{2,1,0:T(1,128)S(1)} %get-tuple-element.58) | copy-start | bytes 12292
  120.0 63.4 %copy-start.26 = (f32[1,1,1024]{2,1,0:T(1,128)}, f32[1,1,1024]{2,1,0:T(1,128)S(1)}, u32[]{:S(2)}) copy-start(f32[1,1,1024]{2,1,0:T(1,128)S(1)} %get-tuple-element.57) | copy-start | bytes 12292
  120.0 236.4 %copy-start.24 = (f32[1,1,1024]{2,1,0:T(1,128)}, f32[1,1,1024]{2,1,0:T(1,128)S(1)}, u32[]{:S(2)}) copy-start(f32[1,1,1024]{2,1,0:T(1,128)S(1)} %get-tuple-element.55) | copy-start | bytes 12292
  233.6 3.6 copy-start.6
  237.2 21.3 %copy-start = (f32[8,512,1024]{2,1,0:T(8,128)}, f32[8,512,1024]{2,1,0:T(8,128)S(1)}, u32[]{:S(2)}) copy-start(f32[8,512,1024]{2,1,0:T(8,128)S(1)} %get-tuple-element.67) | copy-start | bytes 50331652
  245.8 9.1 copy-start.1
  270.7 21.1 %copy-start.32 = (bf16[256]{0:T(256)(128)(2,1)S(1)}, bf16[256]{0:T(256)(128)(2,1)}, u32[]{:S(2)}) copy-start(bf16[256]{0:T(256)(128)(2,1)} %param.22) | copy-start | bytes 1540
  270.7 21.1 %copy-start.28 = (u32[32]{0:T(128)S(1)}, u32[32]{0:T(128)}, u32[]{:S(2)}) copy-start(u32[32]{0:T(128)} %constant.40) | copy-start | bytes 388
  270.7 22.4 %copy-start.33 = (bf16[64]{0:T(256)(128)(2,1)S(1)}, bf16[64]{0:T(256)(128)(2,1)}, u32[]{:S(2)}) copy-start(bf16[64]{0:T(256)(128)(2,1)} %param.24) | copy-start | bytes 388
  270.7 22.6 %copy-start.34 = (bf16[64]{0:T(256)(128)(2,1)S(1)}, bf16[64]{0:T(256)(128)(2,1)}, u32[]{:S(2)}) copy-start(bf16[64]{0:T(256)(128)(2,1)} %param.20) | copy-start | bytes 388
  275.1 75.0 %copy-start.3 = (bf16[1,512,1024]{2,1,0:T(8,128)(2,1)S(1)}, bf16[1,512,1024]{2,1,0:T(8,128)(2,1)}, u32[]{:S(2)}) copy-start(bf16[1,512,1024]{2,1,0:T(8,128)(2,1)} %param.13) | copy-start | bytes 3145732
  287.3 54.6 %all-to-all-start.1 = ((bf16[2,2,131072]{2,1,0:T(2,128)(2,1)}), bf16[2,2,131072]{2,1,0:T(2,128)(2,1)}, u32[]{:S(2)}, u32[]{:S(2)}) async-start(bf16[2,2,131072]{2,1,0:T(2,128)(2,1)} %reshape.535), calls=%async_computation.1 | async-start | bytes 2097152 | tf_op jit(solution)/shard_map/all_to_all | solution.py:144
  324.1 30.6 %copy-start.20 = (f32[1024]{0:T(1024)}, f32[1024]{0:T(1024)S(1)}, u32[]{:S(2)}) copy-start(f32[1024]{0:T(1024)S(1)} %convert_element_type.179) | copy-start | bytes 12292
  354.7 1.3 copy-start.9
  356.4 12.0 copy-start.31
  368.4 13.3 copy-start.10
  381.7 9.7 copy-start.36
  381.7 10.0 copy-start.29
  391.7 11.5 copy-start.30
  408.4 18.3 %all-to-all-start.2 = ((bf16[1,512,2,512]{3,1,0,2:T(8,128)(2,1)}), bf16[1,512,2,512]{3,1,0,2:T(8,128)(2,1)S(1)}, u32[]{:S(2)}, u32[]{:S(2)}) async-start(bf16[1,512,2,512]{3,1,0,2:T(8,128)(2,1)} %copy.59), calls=%async_computation.2 | async-start | bytes 2097152 | tf_op jit(solution)/shard_map/all_to_all | solution.py:185
  412.0 361.9 %reduce-scatter.10.cloned.1.call-start = ((), (), s32[]{:S(2)}) async-start(), calls=%async_computation.16 | async-start | bytes 4456448 | tf_op jit(solution)/shard_map/reduce_scatter | solution.py:227
  417.0 364.0 %reduce-scatter.8.cloned.1.call-start = ((), (), s32[]{:S(2)}) async-start(), calls=%async_computation.15 | async-start | bytes 13369344 | tf_op jit(solution)/shard_map/reduce_scatter | solution.py:225
  485.0 37.1 %copy-start.7 = (bf16[1,1024,1,1,512]{1,4,3,2,0:T(8,128)(2,1)S(1)}, bf16[1,1024,1,1,512]{1,4,3,2,0:T(8,128)(2,1)}, u32[]{:S(2)}) copy-start(bf16[1,1024,1,1,512]{1,4,3,2,0:T(8,128)(2,1)} %copy.55) | copy-start | bytes 3145732
  590.2 7.9 copy-start.13
  590.2 7.9 copy-start.14
  598.6 41.4 %copy-start.4 = (bf16[1,512,1024]{2,1,0:T(8,128)(2,1)S(1)}, bf16[1,512,1024]{2,1,0:T(8,128)(2,1)}, u32[]{:S(2)}) copy-start(bf16[1,512,1024]{2,1,0:T(8,128)(2,1)} %param.13) | copy-start | bytes 3145732
  598.7 41.4 %copy-start.17 = (f32[1,1,1024]{2,1,0:T(1,128)S(1)}, f32[1,1,1024]{2,1,0:T(1,128)}, u32[]{:S(2)}) copy-start(f32[1,1,1024]{2,1,0:T(1,128)} %copy-done.16) | copy-start | bytes 12292
  598.7 41.4 %copy-start.19 = (f32[512]{0:T(512)S(1)}, f32[512]{0:T(512)}, u32[]{:S(2)}) copy-start(f32[512]{0:T(512)} %copy-done.18) | copy-start | bytes 6148
  598.7 41.4 %copy-start.23 = (f32[512]{0:T(512)S(1)}, f32[512]{0:T(512)}, u32[]{:S(2)}) copy-start(f32[512]{0:T(512)} %copy-done.22) | copy-start | bytes 6148
  598.7 41.4 %copy-start.27 = (f32[1,1,1024]{2,1,0:T(1,128)S(1)}, f32[1,1,1024]{2,1,0:T(1,128)}, u32[]{:S(2)}) copy-start(f32[1,1,1024]{2,1,0:T(1,128)} %copy-done.26) | copy-start | bytes 12292
  638.4 1.6 copy-start.8
  647.0 314.8 %reduce-scatter.14.cloned.1.call-start = ((), (), s32[]{:S(2)}) async-start(), calls=%async_computation.18 | async-start | bytes 17825792 | tf_op jit(solution)/shard_map/reduce_scatter | solution.py:231
  666.3 476.1 %reduce-scatter.12.cloned.1.call-start = ((), (), s32[]{:S(2)}) async-start(), calls=%async_computation.17 | async-start | bytes 17825792 | tf_op jit(solution)/shard_map/reduce_scatter | solution.py:229
  681.8 1.8 copy-start.15
  681.8 598.7 %reduce-scatter.6.cloned.1.call-start = ((), (), s32[]{:S(2)}) async-start(), calls=%async_computation.14 | async-start | bytes 13369344 | tf_op jit(solution)/shard_map/reduce_scatter | solution.py:217
  746.0 8.5 copy-start.5
  746.0 8.5 copy-start.11
  746.0 8.5 copy-start.12
  746.0 8.5 copy-start.21
  773.8 594.3 %all-reduce.13.cloned.1.call-start = ((), (), s32[]{:S(2)}) async-start(), calls=%async_computation.19 | async-start | bytes 6291456 | tf_op jit(solution)/shard_map/psum | solution.py:235
  (2 other events, 1.7 us)
Sparse Core Ops, SparseCore 0:
  10.3 103.2 all-gather.8
  115.9 59.6 all-gather.10
  177.7 40.1 all-gather.12
  219.9 73.0 all-gather.14
  295.0 73.2 all-gather.16
  417.2 72.9 reduce-scatter.9
  647.1 133.9 reduce-scatter.7
  785.2 176.5 reduce-scatter.13
  965.9 176.4 reduce-scatter.11
  1146.3 134.1 reduce-scatter.5
  1283.0 85.1 all-reduce.12
